TPU v7x, 256 devices: a whole 4x4x8 slice. The times are simulated.
256 devices in a mesh: samples: 64 (over z, y, x_lo), vblocks: 4 (over x_hi, core).
Axes of the slice: x: 4 (x_hi: 2, x_lo: 2; x = x_hi * 2 + x_lo), y: 4, z: 8, core: 2. Of those that a mesh axis runs over, the one named last changes fastest.
Arguments:
- genotypes: int32 [65536, 4096], P('samples', 'vblocks'), may hold values from 0 to 2
- typed_mask: int32 [4096], P('vblocks'), may hold values 0 or 1
- z_scores: float32 [1024, 4096], P('samples', 'vblocks'), may hold values from -60 to 60
Outputs:
- solution: float32 [1024, 4096], P('samples', 'vblocks')
- imputed: float32 [1024, 4096], P('samples', 'vblocks')
All inputs are finite; a program needn't handle non-finite values. No bound on the sum of `typed_mask` on one device may be relied on, other than what follows from the above.
Results may differ from a plain program's by a relative error of at most 0.0068.
Values may be sent and summed in bfloat16 or wider, within the bound.
No kernel may reach another device: no remote copies, remote signals or barrier semaphores. Data moves between devices by JAX's collectives and lax.ppermute only.
A program may use at most 64 MiB of HBM per device.

v0:
```python
import jax
import jax.numpy as jnp
from jax import lax
from jax.sharding import PartitionSpec as P

ITERS = 3
RIDGE = 0.1
EPSILON = 1e-05
HIGHEST = lax.Precision.HIGHEST


def passed_along(block, axis, distance):
    devices = range(lax.axis_size(axis))
    route = [(i - distance, i) for i in devices if i - distance in devices]
    return lax.ppermute(block, axis, route)


def contract_rows(first_mat, second_mat):
    return lax.dot_general(
        first_mat, second_mat, (((0,), (0,)), ((), ())), preferred_element_type=jnp.float32
    )


def times_transpose(vector, matrix):
    return lax.dot_general(
        vector,
        matrix,
        (((1,), (1,)), ((), ())),
        precision=HIGHEST,
        preferred_element_type=jnp.float32,
    )


def local_sums(first_vec, second_vec):
    return jnp.sum(first_vec * second_vec, axis=1)


def on_device(genotypes, typed_mask, z_scores):
    samples_dev, block_width = genotypes.shape
    total_samples = samples_dev * lax.axis_size("samples")
    dosage = genotypes.astype(jnp.float32)
    totals, squares = lax.psum(
        (jnp.sum(dosage, axis=0), jnp.sum(dosage * dosage, axis=0)), "samples"
    )
    mean_dosage = totals / total_samples
    variance = squares / total_samples - mean_dosage * mean_dosage
    standard = ((dosage - mean_dosage) * lax.rsqrt(variance + EPSILON)).astype(jnp.bfloat16)
    following = passed_along(standard, "vblocks", -1)
    joined = jnp.concatenate([standard, following], axis=1)
    summed = lax.psum_scatter(
        contract_rows(standard, joined), "samples", scatter_dimension=0, tiled=True
    )
    link_rows = (summed / total_samples).astype(jnp.bfloat16)
    gathered = lax.all_gather(link_rows, "samples", axis=0, tiled=True)
    own_block = gathered[:, :block_width].astype(jnp.float32)
    edge_half = gathered[:, block_width:]
    edge_block = edge_half.astype(jnp.float32)

    def apply_link(vector):
        ahead_part = passed_along(vector, "vblocks", -1)
        outgoing = jnp.dot(
            vector, edge_block, precision=HIGHEST, preferred_element_type=jnp.float32
        )
        lower_part = passed_along(outgoing, "vblocks", 1)
        result = times_transpose(vector, own_block)
        result = result + 0.5 * times_transpose(ahead_part, edge_block)
        return result + 0.5 * lower_part

    mask_row = typed_mask.astype(jnp.float32)[None, :]
    right_side = mask_row * z_scores
    solution = jnp.zeros_like(right_side)
    residual = right_side

    def squares_sum(vector):
        return lax.psum(local_sums(vector, vector), "vblocks")

    direction = right_side
    norm_now = squares_sum(residual)
    for iteration in range(ITERS):
        image = mask_row * apply_link(mask_row * direction) + RIDGE * direction
        step_size = norm_now / lax.psum(local_sums(direction, image), "vblocks")
        solution = solution + step_size[:, None] * direction
        residual = residual - step_size[:, None] * image
        if iteration + 1 < ITERS:
            norm_next = squares_sum(residual)
            direction = residual + (norm_next / norm_now)[:, None] * direction
            norm_now = norm_next
    projected = apply_link(mask_row * solution)
    imputed = jnp.where(typed_mask[None, :] == 1, z_scores, projected)
    return (solution, imputed)


def solution(mesh):
    placed = (P("samples", "vblocks"), P("vblocks"), P("samples", "vblocks"))
    return jax.shard_map(
        on_device,
        mesh=mesh,
        in_specs=placed,
        out_specs=(P("samples", "vblocks"), P("samples", "vblocks")),
        check_vma=False,
    )
```

profile of v0, /device:TPU:1, one launch (start us, length us, event | category | flops | bytes accessed | tf_op | source)
XLA Modules:
  0.0 945.3 jit_solution(10318953864122489320)
XLA Ops:
  7.2 2.8 convert_reduce_fusion
  10.0 136.7 %all-reduce = (f32[1024]{0:T(1024)S(1)}, f32[1024]{0:T(1024)S(1)}) all-reduce(f32[1024]{0:T(1024)S(1)} %get-tuple-element.3, f32[1024]{0:T(1024)S(1)} %get-tuple-element.2), channel_id=1, replica_groups=mesh['samples'=64,'vblocks'=4] {'samples'}, use_global_device_ids=true, to_apply=%region_5.0 | all-reduce | flops 2048 | bytes 16384 | tf_op jit(solution)/shard_map/psum | solution.py:42
  146.7 2.8 multiply_convert_fusion
  149.5 30.3 %collective-permute-start = (bf16[1024,1024]{1,0:T(8,128)(2,1)S(1)}, bf16[1024,1024]{1,0:T(8,128)(2,1)S(1)}, u32[]{:S(2)}, u32[]{:S(2)}) collective-permute-start(bf16[1024,1024]{1,0:T(8,128)(2,1)S(1)} %multiply_convert_fusion), channel_id=1, source_target_pairs={{1,0},{2,1},{3,2},{5,4},{6,5},{7,6},{9,8},{10,9},{11,10},{13,12},{... | collective-permute-start | bytes 6291464 | tf_op jit(solution)/shard_map/ppermute | solution.py:15
  179.9 26.1 %collective-permute-done = bf16[1024,1024]{1,0:T(8,128)(2,1)S(1)} collective-permute-done((bf16[1024,1024]{1,0:T(8,128)(2,1)S(1)}, bf16[1024,1024]{1,0:T(8,128)(2,1)S(1)}, u32[]{:S(2)}, u32[]{:S(2)}) %collective-permute-start) | collective-permute-done | bytes 2097184 | tf_op jit(solution)/shard_map/ppermute | solution.py:15
  206.0 7.0 fusion
  213.1 280.4 %reduce-scatter.2.cloned.1.call-done = f32[16,2048]{1,0:T(8,128)} async-done(((f32[1024,2048]{1,0:T(8,128)}), f32[16,2048]{1,0:T(8,128)}) %reduce-scatter.2.cloned.1.call-update) | async-done | bytes 131088 | tf_op jit(solution)/shard_map/reduce_scatter | solution.py:50
  495.2 50.4 %collective-permute-start.1 = (f32[16,1024]{1,0:T(8,128)S(1)}, f32[16,1024]{1,0:T(8,128)S(1)}, u32[]{:S(2)}, u32[]{:S(2)}) collective-permute-start(f32[16,1024]{1,0:T(8,128)S(1)} %multiply_multiply_fusion), channel_id=1, source_target_pairs={{1,0},{2,1},{3,2},{5,4},{6,5},{7,6},{9,8},{10,9},{11,10},{13,12},{... | collective-permute-start | bytes 196616 | tf_op jit(solution)/shard_map/ppermute | solution.py:15
  545.5 251.5 %all-gather.2.cloned.1.call-done = bf16[1024,2048]{1,0:T(8,128)(2,1)} async-done(((bf16[16,2048]{1,0:T(8,128)(2,1)}), bf16[1024,2048]{1,0:T(8,128)(2,1)}) %all-gather.2.cloned.1.call-update) | async-done | bytes 4194320 | tf_op jit(solution)/shard_map/all_gather | solution.py:54
  797.1 2.7 fusion.38
  799.7 50.3 %collective-permute-start.2 = (f32[16,1024]{1,0:T(8,128)S(1)}, f32[16,1024]{1,0:T(8,128)S(1)}, u32[]{:S(2)}, u32[]{:S(2)}) collective-permute-start(f32[16,1024]{1,0:T(8,128)S(1)} %fusion.38), channel_id=1, source_target_pairs={{0,1},{1,2},{2,3},{4,5},{5,6},{6,7},{8,9},{9,10},{10,11},{12,13},{... | collective-permute-start | bytes 196616 | tf_op jit(solution)/shard_map/ppermute | solution.py:15
  850.1 3.3 fusion.10
  853.4 1.9 multiply_reduce_fusion.4
  855.3 6.6 all-reduce.1
  862.1 7.6 psum.60
  869.8 4.0 collective-permute-start.3
  873.8 2.5 fusion.35
  876.3 3.6 collective-permute-start.4
  879.9 3.3 fusion.8
  885.1 6.6 psum.61
  891.9 7.6 psum.62
  899.6 4.2 collective-permute-start.5
  903.8 2.5 fusion.32
  906.3 3.6 collective-permute-start.6
  909.9 3.3 fusion.6
  913.2 1.9 fusion.28
  915.1 6.6 psum.63
  922.4 3.1 collective-permute-start.7
  925.5 2.5 fusion.29
  928.0 4.7 collective-permute-start.8
  932.7 3.3 fusion.4
  936.0 2.4 fusion.14
  (40 shorter events, 4.9 us)
Async XLA Ops:
  7.2 486.4 %reduce-scatter.2.cloned.1.call-start = ((), (), s32[]{:S(2)}) async-start(), calls=%async_computation.1 | async-start | bytes 8519680 | tf_op jit(solution)/shard_map/reduce_scatter | solution.py:50
  149.5 56.5 %collective-permute-start = (bf16[1024,1024]{1,0:T(8,128)(2,1)S(1)}, bf16[1024,1024]{1,0:T(8,128)(2,1)S(1)}, u32[]{:S(2)}, u32[]{:S(2)}) collective-permute-start(bf16[1024,1024]{1,0:T(8,128)(2,1)S(1)} %multiply_convert_fusion), channel_id=1, source_target_pairs={{1,0},{2,1},{3,2},{5,4},{6,5},{7,6},{9,8},{10,9},{11,10},{13,12},{... | collective-permute-start | bytes 6291464 | tf_op jit(solution)/shard_map/ppermute | solution.py:15
  213.0 282.1 %copy-start.5 = (s32[1024]{0:T(1024)S(1)}, s32[1024]{0:T(1024)}, u32[]{:S(2)}) copy-start(s32[1024]{0:T(1024)} %param.4) | copy-start | bytes 12292
  213.0 282.1 %copy-start.4 = (f32[16,1024]{1,0:T(8,128)S(1)}, f32[16,1024]{1,0:T(8,128)}, u32[]{:S(2)}) copy-start(f32[16,1024]{1,0:T(8,128)} %param.5) | copy-start | bytes 196612
  213.0 584.0 %all-gather.2.cloned.1.call-start = ((), (), s32[]{:S(2)}) async-start(), calls=%async_computation.2 | async-start | bytes 4259840 | tf_op jit(solution)/shard_map/all_gather | solution.py:54
  495.2 358.2 %collective-permute-start.1 = (f32[16,1024]{1,0:T(8,128)S(1)}, f32[16,1024]{1,0:T(8,128)S(1)}, u32[]{:S(2)}, u32[]{:S(2)}) collective-permute-start(f32[16,1024]{1,0:T(8,128)S(1)} %multiply_multiply_fusion), channel_id=1, source_target_pairs={{1,0},{2,1},{3,2},{5,4},{6,5},{7,6},{9,8},{10,9},{11,10},{13,12},{... | collective-permute-start | bytes 196616 | tf_op jit(solution)/shard_map/ppermute | solution.py:15
  797.0 56.4 %copy-start = (bf16[1024,2048]{1,0:T(8,128)(2,1)S(1)}, bf16[1024,2048]{1,0:T(8,128)(2,1)}, u32[]{:S(2)}) copy-start(bf16[1024,2048]{1,0:T(8,128)(2,1)} %all-gather.2.cloned.1.call-done) | copy-start | bytes 12582916
  799.7 53.7 %collective-permute-start.2 = (f32[16,1024]{1,0:T(8,128)S(1)}, f32[16,1024]{1,0:T(8,128)S(1)}, u32[]{:S(2)}, u32[]{:S(2)}) collective-permute-start(f32[16,1024]{1,0:T(8,128)S(1)} %fusion.38), channel_id=1, source_target_pairs={{0,1},{1,2},{2,3},{4,5},{5,6},{6,7},{8,9},{9,10},{10,11},{12,13},{... | collective-permute-start | bytes 196616 | tf_op jit(solution)/shard_map/ppermute | solution.py:15
  869.7 13.6 %copy-start.1 = (bf16[1024,2048]{1,0:T(8,128)(2,1)S(1)}, bf16[1024,2048]{1,0:T(8,128)(2,1)}, u32[]{:S(2)}) copy-start(bf16[1024,2048]{1,0:T(8,128)(2,1)} %all-gather.2.cloned.1.call-done) | copy-start | bytes 12582916
  869.8 13.4 %collective-permute-start.3 = (f32[16,1024]{1,0:T(8,128)S(1)}, f32[16,1024]{1,0:T(8,128)S(1)}, u32[]{:S(2)}, u32[]{:S(2)}) collective-permute-start(f32[16,1024]{1,0:T(8,128)S(1)} %get-tuple-element.14), channel_id=1, source_target_pairs={{1,0},{2,1},{3,2},{5,4},{6,5},{7,6},{9,8},{10,9},{11,10},{13,12},{... | collective-permute-start | bytes 196616 | tf_op jit(solution)/shard_map/ppermute | solution.py:15
  876.3 6.9 collective-permute-start.4
  899.5 13.7 %copy-start.2 = (bf16[1024,2048]{1,0:T(8,128)(2,1)S(1)}, bf16[1024,2048]{1,0:T(8,128)(2,1)}, u32[]{:S(2)}) copy-start(bf16[1024,2048]{1,0:T(8,128)(2,1)} %all-gather.2.cloned.1.call-done) | copy-start | bytes 12582916
  899.6 13.6 %collective-permute-start.5 = (f32[16,1024]{1,0:T(8,128)S(1)}, f32[16,1024]{1,0:T(8,128)S(1)}, u32[]{:S(2)}, u32[]{:S(2)}) collective-permute-start(f32[16,1024]{1,0:T(8,128)S(1)} %get-tuple-element.12), channel_id=1, source_target_pairs={{1,0},{2,1},{3,2},{5,4},{6,5},{7,6},{9,8},{10,9},{11,10},{13,12},{... | collective-permute-start | bytes 196616 | tf_op jit(solution)/shard_map/ppermute | solution.py:15
  906.3 6.9 collective-permute-start.6
  921.7 14.3 %copy-start.3 = (bf16[1024,2048]{1,0:T(8,128)(2,1)S(1)}, bf16[1024,2048]{1,0:T(8,128)(2,1)}, u32[]{:S(2)}) copy-start(bf16[1024,2048]{1,0:T(8,128)(2,1)} %all-gather.2.cloned.1.call-done) | copy-start | bytes 12582916
  922.4 13.6 %collective-permute-start.7 = (f32[16,1024]{1,0:T(8,128)S(1)}, f32[16,1024]{1,0:T(8,128)S(1)}, u32[]{:S(2)}, u32[]{:S(2)}) collective-permute-start(f32[16,1024]{1,0:T(8,128)S(1)} %get-tuple-element.10), channel_id=1, source_target_pairs={{1,0},{2,1},{3,2},{5,4},{6,5},{7,6},{9,8},{10,9},{11,10},{13,12},{... | collective-permute-start | bytes 196616 | tf_op jit(solution)/shard_map/ppermute | solution.py:15
  928.0 8.0 collective-permute-start.8
Sparse Core Ops, SparseCore 0:
  213.2 280.3 reduce-scatter.1
  495.9 301.1 all-gather.1
where the time goes:
time: 946 us; the launch traced here: 945 us
  waiting for transfers between devices  558 us (59%)
  blocking collectives  172 us (18%)
  starting transfers between devices  154 us (16%)
  matrix products  38.4 us (4%)
  between operations  14.3 us (2%)
    reduce_scatter x1, waiting for transfers between devices, on_device(): lax.psum_scatter(contract_rows(standard, joined), 'samples', scatter_dime...  280 us
    all_gather x1, waiting for transfers between devices, on_device(): gathered = lax.all_gather(link_rows, 'samples', axis=0, tiled=True)  252 us
    ppermute x9, starting transfers between devices, passed_along(): return lax.ppermute(block, axis, route)  154 us
    psum x1, blocking collectives, on_device(): lax.psum((jnp.sum(dosage, axis=0), jnp.sum(dosage * dosage, axis=0)), 'sa...  137 us
    ppermute x9, waiting for transfers between devices, passed_along(): return lax.ppermute(block, axis, route)  26.2 us
    psum x3, blocking collectives, squares_sum(): return lax.psum(local_sums(vector, vector), 'vblocks')  21.8 us
    dot_general x8, matrix products, times_transpose(): lax.dot_general(vector, matrix, (((1,), (1,)), ((), ())), precision=HIGHE...  21.2 us
  transfers between devices with their start and end apart: 11, of which 3 were waited for; matrix products, arithmetic and copies ran while one was open for 2% of the time, Pallas kernels for 0%

commit v1 on v0

--- a/solution.py
+++ b/solution.py
@@ -51,7 +51,9 @@
         contract_rows(standard, joined), "samples", scatter_dimension=0, tiled=True
     )
     link_rows = (summed / total_samples).astype(jnp.bfloat16)
-    gathered = lax.all_gather(link_rows, "samples", axis=0, tiled=True)
+    gathered = jnp.concatenate(
+        lax.all_to_all(jnp.stack([link_rows] * lax.axis_size("samples")), "samples", 0, 0), axis=0
+    )
     own_block = gathered[:, :block_width].astype(jnp.float32)
     edge_half = gathered[:, block_width:]
     edge_block = edge_half.astype(jnp.float32)

time: 946 us -> 722 us (0.76)
  waiting for transfers between devices: 558 us -> 308 us
  starting transfers between devices: 154 us -> 172 us
    all_gather x1 -> x0, waiting for transfers between devices: 252 us -> none  [on_device(): gathered = lax.all_gather(link_rows, 'samples', axis=0, tiled=True)]
    ppermute x9, starting transfers between devices: 154 us -> 166 us  [passed_along(): return lax.ppermute(block, axis, route)]
  transfers between devices with their start and end apart: 11 -> 11, of which waited for: 3 -> 2; matrix products, arithmetic and copies ran while one was open for 2% -> 2% of each run, Pallas kernels for 0% -> 0%
where the time goes in v1:
time: 722 us; the launch traced here: 721 us
  waiting for transfers between devices  308 us (43%)
  starting transfers between devices  172 us (24%)
  blocking collectives  172 us (24%)
  matrix products  44.6 us (6%)
  between operations  14.3 us (2%)
  other arithmetic  7.86 us (1%)
    reduce_scatter x1, waiting for transfers between devices, on_device(): lax.psum_scatter(contract_rows(standard, joined), 'samples', scatter_dime...  282 us
    ppermute x9, starting transfers between devices, passed_along(): return lax.ppermute(block, axis, route)  166 us
    psum x1, blocking collectives, on_device(): lax.psum((jnp.sum(dosage, axis=0), jnp.sum(dosage * dosage, axis=0)), 'sa...  137 us
    dot_general x8, matrix products, times_transpose(): lax.dot_general(vector, matrix, (((1,), (1,)), ((), ())), precision=HIGHE...  27.6 us
    ppermute x9, waiting for transfers between devices, passed_along(): return lax.ppermute(block, axis, route)  26.2 us
    psum x3, blocking collectives, squares_sum(): return lax.psum(local_sums(vector, vector), 'vblocks')  21.8 us
  transfers between devices with their start and end apart: 11, of which 2 were waited for; matrix products, arithmetic and copies ran while one was open for 2% of the time, Pallas kernels for 0%

profile of v1, /device:TPU:1, one launch (start us, length us, event | category | flops | bytes accessed | tf_op | source)
XLA Modules:
  0.0 721.0 jit_solution(14772173988426731205)
XLA Ops:
  7.2 2.8 convert_reduce_fusion
  10.0 136.7 %all-reduce = (f32[1024]{0:T(1024)S(1)}, f32[1024]{0:T(1024)S(1)}) all-reduce(f32[1024]{0:T(1024)S(1)} %get-tuple-element.3, f32[1024]{0:T(1024)S(1)} %get-tuple-element.2), channel_id=1, replica_groups=mesh['samples'=64,'vblocks'=4] {'samples'}, use_global_device_ids=true, to_apply=%region_5.0 | all-reduce | flops 2048 | bytes 16384 | tf_op jit(solution)/shard_map/psum | solution.py:42
  146.7 2.8 multiply_convert_fusion
  149.5 30.3 %collective-permute-start = (bf16[1024,1024]{1,0:T(8,128)(2,1)S(1)}, bf16[1024,1024]{1,0:T(8,128)(2,1)S(1)}, u32[]{:S(2)}, u32[]{:S(2)}) collective-permute-start(bf16[1024,1024]{1,0:T(8,128)(2,1)S(1)} %multiply_convert_fusion), channel_id=1, source_target_pairs={{1,0},{2,1},{3,2},{5,4},{6,5},{7,6},{9,8},{10,9},{11,10},{13,12},{... | collective-permute-start | bytes 6291464 | tf_op jit(solution)/shard_map/ppermute | solution.py:15
  179.9 26.1 %collective-permute-done = bf16[1024,1024]{1,0:T(8,128)(2,1)S(1)} collective-permute-done((bf16[1024,1024]{1,0:T(8,128)(2,1)S(1)}, bf16[1024,1024]{1,0:T(8,128)(2,1)S(1)}, u32[]{:S(2)}, u32[]{:S(2)}) %collective-permute-start) | collective-permute-done | bytes 2097184 | tf_op jit(solution)/shard_map/ppermute | solution.py:15
  206.0 7.0 fusion
  213.0 281.8 %reduce-scatter.2.cloned.1.call-done = f32[16,2048]{1,0:T(8,128)} async-done(((f32[1024,2048]{1,0:T(8,128)}), f32[16,2048]{1,0:T(8,128)}) %reduce-scatter.2.cloned.1.call-update) | async-done | bytes 131088 | tf_op jit(solution)/shard_map/reduce_scatter | solution.py:50
  498.2 5.8 all-to-all-start
  504.1 58.0 %collective-permute-start.1 = (f32[16,1024]{1,0:T(8,128)S(1)}, f32[16,1024]{1,0:T(8,128)S(1)}, u32[]{:S(2)}, u32[]{:S(2)}) collective-permute-start(f32[16,1024]{1,0:T(8,128)S(1)} %multiply_multiply_fusion), channel_id=1, source_target_pairs={{1,0},{2,1},{3,2},{5,4},{6,5},{7,6},{9,8},{10,9},{11,10},{13,12},{... | collective-permute-start | bytes 196616 | tf_op jit(solution)/shard_map/ppermute | solution.py:15
  562.1 2.5 fusion.38
  564.6 55.5 %collective-permute-start.2 = (f32[16,1024]{1,0:T(8,128)S(1)}, f32[16,1024]{1,0:T(8,128)S(1)}, u32[]{:S(2)}, u32[]{:S(2)}) collective-permute-start(f32[16,1024]{1,0:T(8,128)S(1)} %fusion.38), channel_id=1, source_target_pairs={{0,1},{1,2},{2,3},{4,5},{5,6},{6,7},{8,9},{9,10},{10,11},{12,13},{... | collective-permute-start | bytes 196616 | tf_op jit(solution)/shard_map/ppermute | solution.py:15
  620.1 3.3 fusion.10
  623.5 3.4 multiply_reduce_fusion.4
  626.9 6.6 all-reduce.1
  633.8 7.6 %psum.60 = f32[16]{0:T(128)S(1)} all-reduce(f32[16]{0:T(128)S(1)} %get-tuple-element.16), channel_id=1, replica_groups=mesh['samples'=64,'vblocks'=4] {'vblocks'}, use_global_device_ids=true, to_apply=%region_10.0 | all-reduce | flops 16 | bytes 128 | tf_op jit(solution)/shard_map/psum | solution.py:77
  641.4 2.5 fusion.35
  643.9 3.7 collective-permute-start.3
  647.7 3.8 collective-permute-start.4
  651.4 3.3 fusion.8
  654.8 3.4 multiply_reduce_fusion.2
  658.2 6.6 psum.61
  665.1 7.6 %psum.62 = f32[16]{0:T(128)S(1)} all-reduce(f32[16]{0:T(128)S(1)} %multiply_reduce_fusion.1), channel_id=1, replica_groups=mesh['samples'=64,'vblocks'=4] {'vblocks'}, use_global_device_ids=true, to_apply=%region_14.0 | all-reduce | flops 16 | bytes 128 | tf_op jit(solution)/shard_map/psum | solution.py:77
  672.7 2.5 fusion.32
  675.3 3.6 collective-permute-start.5
  678.8 3.8 collective-permute-start.6
  682.6 3.3 fusion.6
  685.9 3.4 fusion.28
  689.4 6.6 psum.63
  699.2 2.9 collective-permute-start.7
  702.2 4.7 collective-permute-start.8
  706.9 3.3 fusion.4
  710.2 4.0 fusion.14
  (32 shorter events, 7.4 us)
Async XLA Ops:
  7.2 487.7 %reduce-scatter.2.cloned.1.call-start = ((), (), s32[]{:S(2)}) async-start(), calls=%async_computation.2 | async-start | bytes 8519680 | tf_op jit(solution)/shard_map/reduce_scatter | solution.py:50
  149.5 56.5 %collective-permute-start = (bf16[1024,1024]{1,0:T(8,128)(2,1)S(1)}, bf16[1024,1024]{1,0:T(8,128)(2,1)S(1)}, u32[]{:S(2)}, u32[]{:S(2)}) collective-permute-start(bf16[1024,1024]{1,0:T(8,128)(2,1)S(1)} %multiply_convert_fusion), channel_id=1, source_target_pairs={{1,0},{2,1},{3,2},{5,4},{6,5},{7,6},{9,8},{10,9},{11,10},{13,12},{... | collective-permute-start | bytes 6291464 | tf_op jit(solution)/shard_map/ppermute | solution.py:15
  498.2 5.8 copy-start.1
  498.2 5.8 copy-start
  498.2 63.9 %all-to-all-start = ((bf16[64,16,2048]{2,1,0:T(8,128)(2,1)}), bf16[64,16,2048]{2,1,0:T(8,128)(2,1)}, u32[]{:S(2)}, u32[]{:S(2)}) async-start(bf16[64,16,2048]{2,1,0:T(8,128)(2,1)} %stack.2), calls=%async_computation.1 | async-start | bytes 8388608 | tf_op jit(solution)/shard_map/all_to_all | solution.py:55
  504.1 119.4 %collective-permute-start.1 = (f32[16,1024]{1,0:T(8,128)S(1)}, f32[16,1024]{1,0:T(8,128)S(1)}, u32[]{:S(2)}, u32[]{:S(2)}) collective-permute-start(f32[16,1024]{1,0:T(8,128)S(1)} %multiply_multiply_fusion), channel_id=1, source_target_pairs={{1,0},{2,1},{3,2},{5,4},{6,5},{7,6},{9,8},{10,9},{11,10},{13,12},{... | collective-permute-start | bytes 196616 | tf_op jit(solution)/shard_map/ppermute | solution.py:15
  564.6 58.8 %collective-permute-start.2 = (f32[16,1024]{1,0:T(8,128)S(1)}, f32[16,1024]{1,0:T(8,128)S(1)}, u32[]{:S(2)}, u32[]{:S(2)}) collective-permute-start(f32[16,1024]{1,0:T(8,128)S(1)} %fusion.38), channel_id=1, source_target_pairs={{0,1},{1,2},{2,3},{4,5},{5,6},{6,7},{8,9},{9,10},{10,11},{12,13},{... | collective-permute-start | bytes 196616 | tf_op jit(solution)/shard_map/ppermute | solution.py:15
  643.9 10.8 %collective-permute-start.3 = (f32[16,1024]{1,0:T(8,128)S(1)}, f32[16,1024]{1,0:T(8,128)S(1)}, u32[]{:S(2)}, u32[]{:S(2)}) collective-permute-start(f32[16,1024]{1,0:T(8,128)S(1)} %get-tuple-element.14), channel_id=1, source_target_pairs={{1,0},{2,1},{3,2},{5,4},{6,5},{7,6},{9,8},{10,9},{11,10},{13,12},{... | collective-permute-start | bytes 196616 | tf_op jit(solution)/shard_map/ppermute | solution.py:15
  647.7 7.1 collective-permute-start.4
  675.3 10.7 %collective-permute-start.5 = (f32[16,1024]{1,0:T(8,128)S(1)}, f32[16,1024]{1,0:T(8,128)S(1)}, u32[]{:S(2)}, u32[]{:S(2)}) collective-permute-start(f32[16,1024]{1,0:T(8,128)S(1)} %get-tuple-element.12), channel_id=1, source_target_pairs={{1,0},{2,1},{3,2},{5,4},{6,5},{7,6},{9,8},{10,9},{11,10},{13,12},{... | collective-permute-start | bytes 196616 | tf_op jit(solution)/shard_map/ppermute | solution.py:15
  678.8 7.1 collective-permute-start.6
  699.2 11.0 %collective-permute-start.7 = (f32[16,1024]{1,0:T(8,128)S(1)}, f32[16,1024]{1,0:T(8,128)S(1)}, u32[]{:S(2)}, u32[]{:S(2)}) collective-permute-start(f32[16,1024]{1,0:T(8,128)S(1)} %get-tuple-element.10), channel_id=1, source_target_pairs={{1,0},{2,1},{3,2},{5,4},{6,5},{7,6},{9,8},{10,9},{11,10},{13,12},{... | collective-permute-start | bytes 196616 | tf_op jit(solution)/shard_map/ppermute | solution.py:15
  702.2 8.0 %collective-permute-start.8 = (f32[16,1024]{1,0:T(8,128)S(1)}, f32[16,1024]{1,0:T(8,128)S(1)}, u32[]{:S(2)}, u32[]{:S(2)}) collective-permute-start(f32[16,1024]{1,0:T(8,128)S(1)} %fusion.29), channel_id=1, source_target_pairs={{0,1},{1,2},{2,3},{4,5},{5,6},{6,7},{8,9},{9,10},{10,11},{12,13},{... | collective-permute-start | bytes 196616 | tf_op jit(solution)/shard_map/ppermute | solution.py:15
Sparse Core Ops, SparseCore 0:
  213.1 281.6 reduce-scatter.1
